TPU v7x, 256 devices: a whole 4x4x8 slice. The times are simulated.
256 devices in a mesh: dst: 32 (over y, z), src: 8 (over x, core).
Axes of the slice: x: 4, y: 4, z: 8, core: 2. Of those that a mesh axis runs over, the one named last changes fastest.
Arguments:
- transitions: bfloat16 [16384, 128, 128], P(('dst', 'src')), may hold values from 0.0009994507 to 1
- row_block: int32 [16384], P(('dst', 'src')), may hold values from -1 to 1023, as said below
- col_block: int32 [16384], P(('dst', 'src')), may hold values from -1 to 1023, as said below
- beta_last: float32 [32, 128, 8, 128], P(None, 'dst', 'src'), may hold values from 0.2 to 2
- emissions: bfloat16 [2, 32, 128, 8, 128], P(None, None, 'dst', 'src'), may hold values from 0.019897461 to 1
- forward: bfloat16 [2, 32, 128, 8, 128], P(None, None, 'dst', 'src'), may hold values from 0.03 to 125, as said below
Outputs:
- counts: bfloat16 [16384, 128, 128], P(('dst', 'src'))
- beta_first: float32 [32, 128, 8, 128], P(None, 'dst', 'src')
- log_norms: float32 [2, 32], replicated
Inputs may be any that keep to these rules, and one draw needn't show every extreme that they name: `row_block`: slots are grouped by device (index dst * 8 + src), 64 to a device. A live slot holds a block whose source block number r has r % 8 equal to the device's src index and whose destination block lies in the device's dst index's own consecutive equal share of blocks; no block appears twice; live slots come first, and empty ones hold -1 in both arrays. One device has all 64 slots live; each device has at least one. `col_block`: same slots as row_block; -1 exactly where row_block is -1. `forward`: Positive.
All inputs are finite; a program needn't handle non-finite values.
Results may differ from a plain program's by a relative error of at most 0.0029.
Values may be sent and summed in bfloat16 or wider, within the bound.
No kernel may reach another device: no remote copies, remote signals or barrier semaphores. Data moves between devices by JAX's collectives and lax.ppermute only.
A program may use at most 64 MiB of HBM per device.

v0:
```python
import jax
import jax.numpy as jnp
from jax import lax
from jax.sharding import PartitionSpec as P

S = 131072
STEPS = 2


def body(transitions, row_block, col_block, beta_last, emissions, forward):
    source_count = lax.axis_size("src")
    seq_count = beta_last.shape[0]
    local_rows = beta_last.shape[1]
    block_size = beta_last.shape[3]
    slot_count = transitions.shape[0]
    column_count = local_rows * source_count
    total_rows = local_rows * lax.axis_size("dst")
    living = row_block >= 0
    live_float = living.astype(jnp.float32)
    row_local = jnp.where(living, row_block // source_count, 0)
    col_local = jnp.where(living, col_block % column_count, 0)
    beta_piece = beta_last[:, :, 0, :]
    count_sum = jnp.zeros((slot_count, block_size, block_size), jnp.float32)
    log_list = []
    for step_index in range(STEPS):
        emitted = emissions[step_index][:, :, 0, :]
        message = (emitted.astype(jnp.float32) * beta_piece).astype(jnp.bfloat16)
        columns = lax.all_gather(message[:, :, None, :], "src", axis=2, tiled=True)
        columns = columns.reshape(seq_count, column_count, block_size)
        alpha_rows = lax.all_gather(forward[step_index], "dst", axis=1, tiled=True)
        alpha_rows = alpha_rows.reshape(seq_count, total_rows, block_size)
        alpha_picked = jnp.take(alpha_rows, row_local, axis=1)
        picked = jnp.take(columns, col_local, axis=1)
        products = jnp.einsum(
            "bcj,cij->cbi", picked, transitions, preferred_element_type=jnp.float32
        )
        products = products * live_float[:, None, None]
        partial_value = jax.ops.segment_sum(products, row_local, num_segments=total_rows)
        raw_sums = lax.psum_scatter(partial_value, "dst", scatter_dimension=0, tiled=True)
        own_alpha = forward[step_index][:, :, 0, :]
        local_term = jnp.einsum(
            "kbr,bkr->b", raw_sums, own_alpha, preferred_element_type=jnp.float32
        )
        scale_now = lax.psum(local_term, ("dst", "src")) / S
        beta_piece = jnp.transpose(raw_sums / scale_now[None, :, None], (1, 0, 2))
        scaled = (columns.astype(jnp.float32) / scale_now[:, None, None]).astype(jnp.bfloat16)
        scaled_picked = jnp.take(scaled, col_local, axis=1)
        count_sum = count_sum + jnp.einsum(
            "bci,bcj->cij", alpha_picked, scaled_picked, preferred_element_type=jnp.float32
        )
        log_list.append(jnp.log(scale_now))
    counts = (count_sum * transitions.astype(jnp.float32) * live_float[:, None, None]).astype(
        jnp.bfloat16
    )
    return (counts, beta_piece[:, :, None, :], jnp.stack(log_list))


def solution(mesh):
    return jax.shard_map(
        body,
        mesh=mesh,
        in_specs=(
            P(("dst", "src"), None, None),
            P(("dst", "src")),
            P(("dst", "src")),
            P(None, "dst", "src", None),
            P(None, None, "dst", "src", None),
            P(None, None, "dst", "src", None),
        ),
        out_specs=(P(("dst", "src"), None, None), P(None, "dst", "src", None), P()),
        check_vma=False,
    )
```

profile of v0, /device:TPU:1, one launch (start us, length us, event | category | flops | bytes accessed | tf_op | source)
XLA Modules:
  0.0 728.8 jit_solution(5440016924613923832)
XLA Ops:
  7.2 0.0 copy-start
  7.2 0.0 reduce-scatter.3.cloned.1.call-start
  7.2 0.8 compare_and_fusion
  8.1 0.0 copy-start.5
  8.1 0.8 fusion.35
  8.9 0.9 fusion.24
  9.7 15.9 %all_gather.13 = bf16[32,4,8,128]{3,0,1,2:T(8,128)(2,1)S(1)} all-gather(bf16[32,4,1,128]{3,0,1,2:T(8,128)(2,1)S(1)} %fusion.24), channel_id=1, replica_groups=mesh['dst'=32,'src'=8] {'src'}, dimensions={2}, use_global_device_ids=true | all-gather | bytes 294912 | tf_op jit(solution)/shard_map/all_gather | solution.py:28
  25.6 0.2 copy.68
  25.8 0.1 copy.34
  25.9 1.4 gather_fusion.1
  27.3 0.0 copy-done
  27.3 2.3 convolution_multiply_fusion.1
  29.6 1.6 broadcast.28.clone
  31.2 0.0 copy-done.5
  31.2 0.0 copy-start.4
  31.2 8.0 %scatter_fusion = f32[128,32,128]{2,1,0:T(8,128)} fusion(f32[128,32,128]{2,1,0:T(8,128)} %broadcast.28.clone, s32[64]{0:T(128)S(1)} %get-tuple-element.28, f32[64,32,128]{2,1,0:T(8,128)S(1)} %convolution_multiply_fusion.1), kind=kCustom, calls=%fused_computation.6 | custom fusion | flops 262144 | bytes 3145984 | tf_op jit(solution)/shard_map/scatter-add | solution.py:38
  39.2 0.0 reduce-scatter.3.cloned.1.call-update
  39.3 0.0 all-gather.8.cloned.1.call-start
  39.3 0.0 copy-done.4
  39.4 0.6 copy.54
  40.0 0.0 all-gather.8.cloned.1.call-update
  40.0 0.0 all-gather.6.cloned.1.call-start
  40.1 0.6 copy.52
  40.7 0.1 all-gather.6.cloned.1.call-update
  40.8 0.0 reduce-scatter.5.cloned.1.call-start
  40.8 213.9 %reduce-scatter.3.cloned.1.call-done = f32[4,32,128]{2,1,0:T(8,128)} async-done(((f32[128,32,128]{2,1,0:T(8,128)}), f32[4,32,128]{2,1,0:T(8,128)}) %reduce-scatter.3.cloned.1.call-update) | async-done | bytes 65552 | tf_op jit(solution)/shard_map/reduce_scatter | solution.py:39
  254.7 1.0 multiply_reduce_fusion.1
  255.7 79.9 %psum.14 = f32[32]{0:T(128)S(1)} all-reduce(f32[32]{0:T(128)S(1)} %multiply_reduce_fusion.1), channel_id=1, replica_groups=mesh['dst'=32,'src'=8] {'dst','src'}, use_global_device_ids=true, to_apply=%region_2.5 | all-reduce | flops 32 | bytes 256 | tf_op jit(solution)/shard_map/psum | solution.py:44
  335.6 0.9 fusion.23
  336.5 12.6 %all-gather.2 = bf16[32,4,1024]{2,0,1:T(8,128)(2,1)S(1)} all-gather(bf16[32,4,128]{2,0,1:T(8,128)(2,1)S(1)} %fusion.23), channel_id=4, replica_groups=mesh['dst'=32,'src'=8] {'src'}, dimensions={2}, use_global_device_ids=true | all-gather | bytes 294912 | tf_op jit(solution)/shard_map/all_gather | solution.py:28
  349.1 0.2 copy.38
  349.3 0.1 reshape.50
  349.4 0.0 copy-start.1
  349.4 0.1 copy.39
  349.5 0.6 copy-done.1
  350.1 1.4 gather_fusion.4
  351.6 0.0 copy-start.6
  351.6 2.3 convolution_multiply_fusion
  353.8 1.6 broadcast.28
  355.4 0.0 copy-done.6
  355.4 8.0 %scatter_fusion.1 = f32[128,32,128]{2,1,0:T(8,128)} fusion(f32[128,32,128]{2,1,0:T(8,128)} %broadcast.28, s32[64]{0:T(128)S(1)} %copy-done.6, f32[64,32,128]{2,1,0:T(8,128)S(1)} %convolution_multiply_fusion), kind=kCustom, calls=%fused_computation.7 | custom fusion | flops 262144 | bytes 3145984 | tf_op jit(solution)/shard_map/scatter-add | solution.py:38
  363.5 0.0 reduce-scatter.5.cloned.1.call-update
  363.5 0.0 all-gather.8.cloned.1.call-done
  363.6 1.9 gather_fusion.3
  365.5 43.8 %all-gather.6.cloned.1.call-done = bf16[1,32,128,1,128]{4,1,3,0,2:T(8,128)(2,1)} async-done(((bf16[1,32,4,1,128]{4,1,3,0,2:T(8,128)(2,1)}), bf16[1,32,128,1,128]{4,1,3,0,2:T(8,128)(2,1)}) %all-gather.6.cloned.1.call-update) | async-done | bytes 1048592 | tf_op jit(solution)/shard_map/all_gather | solution.py:30
  409.3 2.6 gather_fusion
  411.9 0.1 divide_convert_fusion.1
  412.0 1.4 gather_fusion.2
  413.5 216.1 %reduce-scatter.5.cloned.1.call-done = f32[4,32,128]{2,1,0:T(8,128)} async-done(((f32[128,32,128]{2,1,0:T(8,128)}), f32[4,32,128]{2,1,0:T(8,128)}) %reduce-scatter.5.cloned.1.call-update) | async-done | bytes 65552 | tf_op jit(solution)/shard_map/reduce_scatter | solution.py:39
  629.6 1.0 multiply_reduce_fusion
  630.6 0.0 copy-start.2
  630.6 0.0 copy-start.3
  630.6 4.1 fusion.3
  634.7 79.6 %psum.15 = f32[32]{0:T(128)S(1)} all-reduce(f32[32]{0:T(128)S(1)} %multiply_reduce_fusion), channel_id=1, replica_groups=mesh['dst'=32,'src'=8] {'dst','src'}, use_global_device_ids=true, to_apply=%region_5.8 | all-reduce | flops 32 | bytes 256 | tf_op jit(solution)/shard_map/psum | solution.py:44
  714.3 0.0 copy-done.2
  714.3 0.1 divide_convert_fusion
  714.4 0.0 copy-done.3
  714.5 0.1 divide_bitcast_fusion
  714.5 0.7 copy.41
  715.2 1.4 gather_fusion.5
  716.6 0.6 pad_maximum_fusion
  717.2 5.0 multiply_convert_fusion
  (6 shorter events, 0.1 us)
Async XLA Ops:
  7.2 20.2 %copy-start = (bf16[64,128,128]{2,1,0:T(8,128)(2,1)S(1)}, bf16[64,128,128]{2,1,0:T(8,128)(2,1)}, u32[]{:S(2)}) copy-start(bf16[64,128,128]{2,1,0:T(8,128)(2,1)} %param.10) | copy-start | bytes 6291460
  7.2 247.6 %reduce-scatter.3.cloned.1.call-start = ((), (), s32[]{:S(2)}) async-start(), calls=%async_computation.2 | async-start | bytes 2162688 | tf_op jit(solution)/shard_map/reduce_scatter | solution.py:39
  8.1 23.1 %copy-start.5 = (s32[64]{0:T(128)}, s32[64]{0:T(128)S(1)}, u32[]{:S(2)}) copy-start(s32[64]{0:T(128)S(1)} %get-tuple-element.28) | copy-start | bytes 772
  31.2 8.1 %copy-start.4 = (bf16[2,32,4,1,128]{4,2,3,1,0:T(4,128)(2,1)S(1)}, bf16[2,32,4,1,128]{4,2,3,1,0:T(4,128)(2,1)}, u32[]{:S(2)}) copy-start(bf16[2,32,4,1,128]{4,2,3,1,0:T(4,128)(2,1)} %param.15) | copy-start | bytes 196612
  39.3 324.3 %all-gather.8.cloned.1.call-start = ((), (), s32[]{:S(2)}) async-start(), calls=%async_computation.5 | async-start | bytes 1081344 | tf_op jit(solution)/shard_map/all_gather | solution.py:30
  40.0 369.3 %all-gather.6.cloned.1.call-start = ((), (), s32[]{:S(2)}) async-start(), calls=%async_computation.4 | async-start | bytes 1081344 | tf_op jit(solution)/shard_map/all_gather | solution.py:30
  40.8 588.9 %reduce-scatter.5.cloned.1.call-start = ((), (), s32[]{:S(2)}) async-start(), calls=%async_computation.3 | async-start | bytes 2162688 | tf_op jit(solution)/shard_map/reduce_scatter | solution.py:39
  349.4 0.7 copy-start.1
  351.6 3.9 copy-start.6
  630.6 83.8 %copy-start.2 = (bf16[32,32,128]{2,1,0:T(8,128)(2,1)S(1)}, bf16[32,32,128]{2,1,0:T(8,128)(2,1)}, u32[]{:S(2)}) copy-start(bf16[32,32,128]{2,1,0:T(8,128)(2,1)} %copy-done.1) | copy-start | bytes 786436
  630.6 83.9 %copy-start.3 = (f32[4,32,128]{2,1,0:T(8,128)S(1)}, f32[4,32,128]{2,1,0:T(8,128)}, u32[]{:S(2)}) copy-start(f32[4,32,128]{2,1,0:T(8,128)} %reduce-scatter.5.cloned.1.call-done) | copy-start | bytes 196612
Sparse Core Ops, SparseCore 0:
  39.4 215.2 reduce-scatter.2
  257.3 74.8 all-gather.7
  335.4 73.8 all-gather.5
  413.5 216.0 reduce-scatter.4
where the time goes:
time: 730 us; the launch traced here: 729 us
  waiting for transfers between devices  474 us (65%)
  blocking collectives  188 us (26%)
  other arithmetic  21.5 us (3%)
  local copies, waits for them, and re-layouts  17.5 us (2%)
  between operations  13.9 us (2%)
  matrix products  13.7 us (2%)
    reduce_scatter x2, waiting for transfers between devices, body(): lax.psum_scatter(partial_value, 'dst', scatter_dimension=0, tiled=True)  430 us
    psum x2, blocking collectives, body(): scale_now = lax.psum(local_term, ('dst', 'src')) / S  160 us
    all_gather x2, waiting for transfers between devices, body(): alpha_rows = lax.all_gather(forward[step_index], 'dst', axis=1, tiled=True)  43.8 us
    all_gather x2, blocking collectives, body(): columns = lax.all_gather(message[:, :, None, :], 'src', axis=2, tiled=True)  28.5 us
    scatter-add x2, other arithmetic, body(): jax.ops.segment_sum(products, row_local, num_segments=total_rows)  16.1 us
  transfers between devices with their start and end apart: 4, of which 3 were waited for; matrix products, arithmetic and copies ran while one was open for 3% of the time, Pallas kernels for 0%

commit v1 on v0

--- a/solution.py
+++ b/solution.py
@@ -27,7 +27,17 @@
         message = (emitted.astype(jnp.float32) * beta_piece).astype(jnp.bfloat16)
         columns = lax.all_gather(message[:, :, None, :], "src", axis=2, tiled=True)
         columns = columns.reshape(seq_count, column_count, block_size)
-        alpha_rows = lax.all_gather(forward[step_index], "dst", axis=1, tiled=True)
+
+        def move_ends_now(frame):
+            ready = jnp.concatenate(
+                lax.all_to_all(
+                    jnp.stack([frame for _ in range(lax.axis_size("dst"))]), "dst", 0, 0
+                ),
+                axis=1,
+            )
+            return ready
+
+        alpha_rows = move_ends_now(forward[step_index])
         alpha_rows = alpha_rows.reshape(seq_count, total_rows, block_size)
         alpha_picked = jnp.take(alpha_rows, row_local, axis=1)
         picked = jnp.take(columns, col_local, axis=1)

time: 730 us -> 690 us (0.945)
  waiting for transfers between devices: 474 us -> 416 us
  starting transfers between devices: 0.16 us -> 15.1 us
    all_gather x2 -> x0, waiting for transfers between devices: 43.8 us -> none  [body(): alpha_rows = lax.all_gather(forward[step_index], 'dst', axis=1, tiled=True)]
    reduce_scatter x2, waiting for transfers between devices: 430 us -> 388 us  [body(): lax.psum_scatter(partial_value, 'dst', scatter_dimension=0, tiled=True)]
    all_to_all x0 -> x2, waiting for transfers between devices: none -> 27.7 us  [move_ends_now(): lax.all_to_all(jnp.stack([frame for _ in range(lax.axis_size('dst'))]), '...]
    all_to_all x0 -> x2, starting transfers between devices: none -> 15 us  [move_ends_now(): lax.all_to_all(jnp.stack([frame for _ in range(lax.axis_size('dst'))]), '...]
where the time goes in v1:
time: 690 us; the launch traced here: 688 us
  waiting for transfers between devices  416 us (60%)
  blocking collectives  191 us (28%)
  other arithmetic  21.7 us (3%)
  local copies, waits for them, and re-layouts  17.6 us (3%)
  starting transfers between devices  15.1 us (2%)
  between operations  14.2 us (2%)
  matrix products  13.5 us (2%)
    reduce_scatter x2, waiting for transfers between devices, body(): lax.psum_scatter(partial_value, 'dst', scatter_dimension=0, tiled=True)  388 us
    psum x2, blocking collectives, body(): scale_now = lax.psum(local_term, ('dst', 'src')) / S  163 us
    all_gather x2, blocking collectives, body(): columns = lax.all_gather(message[:, :, None, :], 'src', axis=2, tiled=True)  27.9 us
    all_to_all x2, waiting for transfers between devices, move_ends_now(): lax.all_to_all(jnp.stack([frame for _ in range(lax.axis_size('dst'))]), '...  27.7 us
    scatter-add x2, other arithmetic, body(): jax.ops.segment_sum(products, row_local, num_segments=total_rows)  16.1 us
    all_to_all x2, starting transfers between devices, move_ends_now(): lax.all_to_all(jnp.stack([frame for _ in range(lax.axis_size('dst'))]), '...  15 us
  transfers between devices with their start and end apart: 4, of which 3 were waited for; matrix products, arithmetic and copies ran while one was open for 3% of the time, Pallas kernels for 0%

profile of v1, /device:TPU:1, one launch (start us, length us, event | category | flops | bytes accessed | tf_op | source)
XLA Modules:
  0.0 688.2 jit_solution(1062422283150931931)
XLA Ops:
  7.2 0.0 copy-start
  7.2 0.0 reduce-scatter.3.cloned.1.call-start
  7.2 0.8 compare_and_fusion
  8.1 0.0 copy-start.7
  8.1 0.8 fusion.34
  8.9 0.9 fusion.24
  9.7 15.9 %all_gather.6 = bf16[32,4,8,128]{3,0,1,2:T(8,128)(2,1)S(1)} all-gather(bf16[32,4,1,128]{3,0,1,2:T(8,128)(2,1)S(1)} %fusion.24), channel_id=1, replica_groups=mesh['dst'=32,'src'=8] {'src'}, dimensions={2}, use_global_device_ids=true | all-gather | bytes 294912 | tf_op jit(solution)/shard_map/all_gather | solution.py:28
  25.6 0.2 copy.66
  25.8 0.1 copy.33
  25.9 1.4 gather_fusion.1
  27.3 0.0 copy-done
  27.3 2.3 convolution_multiply_fusion.1
  29.6 1.6 broadcast.32.clone
  31.2 0.0 copy-done.7
  31.2 0.0 copy-start.4
  31.2 8.0 %scatter_fusion = f32[128,32,128]{2,1,0:T(8,128)} fusion(f32[128,32,128]{2,1,0:T(8,128)} %broadcast.32.clone, s32[64]{0:T(128)S(1)} %get-tuple-element.28, f32[64,32,128]{2,1,0:T(8,128)S(1)} %convolution_multiply_fusion.1), kind=kCustom, calls=%fused_computation.6 | custom fusion | flops 262144 | bytes 3145984 | tf_op jit(solution)/shard_map/scatter-add | solution.py:48
  39.2 0.0 reduce-scatter.3.cloned.1.call-update
  39.3 0.0 copy-done.4
  39.3 215.4 %reduce-scatter.3.cloned.1.call-done = f32[4,32,128]{2,1,0:T(8,128)} async-done(((f32[128,32,128]{2,1,0:T(8,128)}), f32[4,32,128]{2,1,0:T(8,128)}) %reduce-scatter.3.cloned.1.call-update) | async-done | bytes 65552 | tf_op jit(solution)/shard_map/reduce_scatter | solution.py:49
  254.7 1.2 multiply_reduce_fusion.1
  256.0 1.3 stack.15
  257.2 6.7 all-to-all-start
  263.9 0.0 reduce-scatter.5.cloned.1.call-start
  263.9 83.0 %psum.14 = f32[32]{0:T(128)S(1)} all-reduce(f32[32]{0:T(128)S(1)} %multiply_reduce_fusion.1), channel_id=1, replica_groups=mesh['dst'=32,'src'=8] {'dst','src'}, use_global_device_ids=true, to_apply=%region_2.5 | all-reduce | flops 32 | bytes 256 | tf_op jit(solution)/shard_map/psum | solution.py:54
  346.9 0.5 log_bitcast_fusion.1
  347.4 0.0 copy-done.6
  347.4 0.1 fusion.23
  347.5 12.0 %all-gather = bf16[32,4,1024]{2,0,1:T(8,128)(2,1)S(1)} all-gather(bf16[32,4,128]{2,0,1:T(8,128)(2,1)S(1)} %fusion.23), channel_id=2, replica_groups=mesh['dst'=32,'src'=8] {'src'}, dimensions={2}, use_global_device_ids=true | all-gather | bytes 294912 | tf_op jit(solution)/shard_map/all_gather | solution.py:28
  359.6 0.0 copy-done.9
  359.6 0.2 copy.38
  359.8 0.1 reshape.56
  359.9 0.0 copy-start.1
  359.9 0.1 copy.39
  360.0 0.6 copy-done.1
  360.6 1.4 gather_fusion.4
  362.0 2.3 convolution_multiply_fusion
  364.3 1.6 broadcast.32
  365.9 0.0 copy-done.8
  365.9 8.0 %scatter_fusion.1 = f32[128,32,128]{2,1,0:T(8,128)} fusion(f32[128,32,128]{2,1,0:T(8,128)} %broadcast.32, s32[64]{0:T(128)S(1)} %copy-done.8, f32[64,32,128]{2,1,0:T(8,128)S(1)} %convolution_multiply_fusion), kind=kCustom, calls=%fused_computation.7 | custom fusion | flops 262144 | bytes 3145984 | tf_op jit(solution)/shard_map/scatter-add | solution.py:48
  373.9 0.0 reduce-scatter.5.cloned.1.call-update
  373.9 0.0 all-to-all-done
  373.9 1.3 stack.16
  375.2 8.4 %all-to-all-start.1 = ((bf16[32,32,4,1,128]{4,1,2,3,0:T(8,128)(2,1)}), bf16[32,32,4,1,128]{4,1,2,3,0:T(8,128)(2,1)S(1)}, u32[]{:S(2)}, u32[]{:S(2)}) async-start(bf16[32,32,4,1,128]{4,1,2,3,0:T(8,128)(2,1)} %stack.16), calls=%async_computation.2 | async-start | bytes 2097152 | tf_op jit(solution)/shard_map/all_to_all | solution.py:33
  383.6 2.7 gather_fusion
  386.3 27.7 %all-to-all-done.1 = bf16[32,32,4,1,128]{4,1,2,3,0:T(8,128)(2,1)S(1)} async-done(((bf16[32,32,4,1,128]{4,1,2,3,0:T(8,128)(2,1)}), bf16[32,32,4,1,128]{4,1,2,3,0:T(8,128)(2,1)S(1)}, u32[]{:S(2)}, u32[]{:S(2)}) %all-to-all-start.1) | async-done | bytes 1048608 | tf_op jit(solution)/shard_map/all_to_all | solution.py:33
  414.0 1.4 gather_fusion.3
  415.4 0.0 copy-done.10
  415.4 0.1 divide_convert_fusion.1
  415.6 0.7 gather_fusion.2
  416.2 172.4 %reduce-scatter.5.cloned.1.call-done = f32[4,32,128]{2,1,0:T(8,128)} async-done(((f32[128,32,128]{2,1,0:T(8,128)}), f32[4,32,128]{2,1,0:T(8,128)}) %reduce-scatter.5.cloned.1.call-update) | async-done | bytes 65552 | tf_op jit(solution)/shard_map/reduce_scatter | solution.py:49
  588.6 1.2 multiply_reduce_fusion
  589.8 0.0 copy-start.11
  589.8 3.9 fusion.3
  593.7 79.7 %psum.15 = f32[32]{0:T(128)S(1)} all-reduce(f32[32]{0:T(128)S(1)} %multiply_reduce_fusion), channel_id=1, replica_groups=mesh['dst'=32,'src'=8] {'dst','src'}, use_global_device_ids=true, to_apply=%region_5.8 | all-reduce | flops 32 | bytes 256 | tf_op jit(solution)/shard_map/psum | solution.py:54
  673.4 0.0 copy-done.2
  673.4 0.1 divide_convert_fusion
  673.5 0.0 copy-done.5
  673.5 0.1 divide_bitcast_fusion
  673.6 0.7 copy.41
  674.3 1.4 gather_fusion.5
  675.7 0.0 copy-done.11
  675.7 0.6 pad_maximum_fusion
  676.3 0.0 copy-done.3
  676.3 5.0 multiply_convert_fusion
  (14 shorter events, 0.1 us)
Async XLA Ops:
  7.2 20.2 %copy-start = (bf16[64,128,128]{2,1,0:T(8,128)(2,1)S(1)}, bf16[64,128,128]{2,1,0:T(8,128)(2,1)}, u32[]{:S(2)}) copy-start(bf16[64,128,128]{2,1,0:T(8,128)(2,1)} %param.10) | copy-start | bytes 6291460
  7.2 247.5 %reduce-scatter.3.cloned.1.call-start = ((), (), s32[]{:S(2)}) async-start(), calls=%async_computation.4 | async-start | bytes 2162688 | tf_op jit(solution)/shard_map/reduce_scatter | solution.py:49
  8.1 23.1 %copy-start.7 = (s32[64]{0:T(128)}, s32[64]{0:T(128)S(1)}, u32[]{:S(2)}) copy-start(s32[64]{0:T(128)S(1)} %get-tuple-element.28) | copy-start | bytes 772
  31.2 8.1 %copy-start.4 = (bf16[2,32,4,1,128]{4,2,3,1,0:T(4,128)(2,1)S(1)}, bf16[2,32,4,1,128]{4,2,3,1,0:T(4,128)(2,1)}, u32[]{:S(2)}) copy-start(bf16[2,32,4,1,128]{4,2,3,1,0:T(4,128)(2,1)} %param.15) | copy-start | bytes 196612
  254.7 92.7 %copy-start.6 = (f32[4,32,128]{2,1,0:T(8,128)S(1)}, f32[4,32,128]{2,1,0:T(8,128)}, u32[]{:S(2)}) copy-start(f32[4,32,128]{2,1,0:T(8,128)} %reduce-scatter.3.cloned.1.call-done) | copy-start | bytes 196612
  257.2 116.7 %all-to-all-start = ((bf16[32,32,4,1,128]{4,1,2,3,0:T(8,128)(2,1)}), bf16[32,32,4,1,128]{4,1,2,3,0:T(8,128)(2,1)}, u32[]{:S(2)}, u32[]{:S(2)}) async-start(bf16[32,32,4,1,128]{4,1,2,3,0:T(8,128)(2,1)} %stack.15), calls=%async_computation | async-start | bytes 2097152 | tf_op jit(solution)/shard_map/all_to_all | solution.py:33
  263.9 324.7 %reduce-scatter.5.cloned.1.call-start = ((), (), s32[]{:S(2)}) async-start(), calls=%async_computation.5 | async-start | bytes 2162688 | tf_op jit(solution)/shard_map/reduce_scatter | solution.py:49
  347.4 12.1 %copy-start.9 = (f32[32]{0:T(128)}, f32[32]{0:T(128)S(1)}, u32[]{:S(2)}) copy-start(f32[32]{0:T(128)S(1)} %get-tuple-element.23) | copy-start | bytes 388
  359.9 0.7 copy-start.1
  362.0 3.9 copy-start.8
  375.2 40.2 %copy-start.10 = (f32[32]{0:T(128)S(1)}, f32[32]{0:T(128)}, u32[]{:S(2)}) copy-start(f32[32]{0:T(128)} %copy-done.9) | copy-start | bytes 388
  375.2 38.8 %all-to-all-start.1 = ((bf16[32,32,4,1,128]{4,1,2,3,0:T(8,128)(2,1)}), bf16[32,32,4,1,128]{4,1,2,3,0:T(8,128)(2,1)S(1)}, u32[]{:S(2)}, u32[]{:S(2)}) async-start(bf16[32,32,4,1,128]{4,1,2,3,0:T(8,128)(2,1)} %stack.16), calls=%async_computation.2 | async-start | bytes 2097152 | tf_op jit(solution)/shard_map/all_to_all | solution.py:33
  589.8 83.6 %copy-start.2 = (bf16[32,32,128]{2,1,0:T(8,128)(2,1)S(1)}, bf16[32,32,128]{2,1,0:T(8,128)(2,1)}, u32[]{:S(2)}) copy-start(bf16[32,32,128]{2,1,0:T(8,128)(2,1)} %copy-done.1) | copy-start | bytes 786436
  589.8 83.8 %copy-start.5 = (f32[4,32,128]{2,1,0:T(8,128)S(1)}, f32[4,32,128]{2,1,0:T(8,128)}, u32[]{:S(2)}) copy-start(f32[4,32,128]{2,1,0:T(8,128)} %reduce-scatter.5.cloned.1.call-done) | copy-start | bytes 196612
  589.8 86.0 %copy-start.11 = (f32[1,32]{1,0:T(1,128)S(1)}, f32[1,32]{1,0:T(1,128)}, u32[]{:S(2)}) copy-start(f32[1,32]{1,0:T(1,128)} %get-tuple-element.22) | copy-start | bytes 388
  593.7 82.6 %copy-start.3 = (bf16[64,32,128]{2,1,0:T(8,128)(2,1)S(1)}, bf16[64,32,128]{2,1,0:T(8,128)(2,1)}, u32[]{:S(2)}) copy-start(bf16[64,32,128]{2,1,0:T(8,128)(2,1)} %gather_fusion.3) | copy-start | bytes 1572868
Sparse Core Ops, SparseCore 0:
  39.4 215.2 reduce-scatter.2
  374.0 214.5 reduce-scatter.4
